TPU v7x, 32 devices: a whole 2x2x4 slice. The times are simulated.
32 devices in a mesh: dp: 8 (over y, x, core), tensor: 4 (over z).
Axes of the slice: x: 2, y: 2, z: 4, core: 2. Of those that a mesh axis runs over, the one named last changes fastest.
Arguments:
- short_tokens: bfloat16 [16, 256, 768], P('dp'), may hold values from -6 to 6
- short_lengths: int32 [16], P('dp'), may hold values from 64 to 256, as said below
- long_tokens: bfloat16 [24, 512, 768], P('dp'), may hold values from -6 to 6
- long_lengths: int32 [24], P('dp'), may hold values from 257 to 512, as said below
- w_qkv: bfloat16 [3, 768, 768], P(None, None, 'tensor'), may hold values from -0.21875 to 0.21875
- b_qv: bfloat16 [2, 12, 64], P(None, 'tensor'), may hold values from -3 to 3
- w_out: bfloat16 [768, 768], P('tensor'), may hold values from -2.5 to 2.5
- res_biases: bfloat16 [2, 768], replicated, may hold values from -3 to 3
- ln_gains: bfloat16 [2, 768], replicated, may hold values from 0.099609375 to 1.8984375
- ln_shifts: bfloat16 [2, 768], replicated, may hold values from -3 to 3
- w_up: bfloat16 [768, 3072], P(None, 'tensor'), may hold values from -0.21875 to 0.21875
- b_up: bfloat16 [4, 768], P('tensor'), may hold values from -3 to 3
- w_down: bfloat16 [3072, 768], P('tensor'), may hold values from -0.109375 to 0.109375
- short_cotangent: bfloat16 [16, 256, 768], P('dp'), may hold values from -6 to 6
- long_cotangent: bfloat16 [24, 512, 768], P('dp'), may hold values from -6 to 6
Outputs:
- short_encoded: bfloat16 [16, 256, 768], P('dp')
- long_encoded: bfloat16 [24, 512, 768], P('dp')
- short_grad_tokens: float32 [16, 256, 768], P('dp')
- long_grad_tokens: float32 [24, 512, 768], P('dp')
- grad_qkv: float32 [3, 768, 768], P(None, 'dp', 'tensor')
- grad_qv_bias: float32 [2, 12, 64], P(None, 'tensor', 'dp')
- grad_out: float32 [768, 768], P('tensor', 'dp')
- grad_res_biases: float32 [2, 768], P(None, 'dp')
- grad_gains: float32 [2, 768], P(None, 'dp')
- grad_shifts: float32 [2, 768], P(None, 'dp')
- grad_up: float32 [768, 3072], P('dp', 'tensor')
- grad_up_bias: float32 [4, 768], P('tensor', 'dp')
- grad_down: float32 [3072, 768], P('tensor', 'dp')
Inputs may be any that keep to these rules, and one draw needn't show every extreme that they name: `short_lengths`: the first short pair has 256 valid tokens. `long_lengths`: the first long pair has 512 valid tokens.
All inputs are finite; a program needn't handle non-finite values.
Results may differ from a plain program's by a relative error of at most 0.013.
The roundings to bfloat16 on the way count: a program that leaves them out, or rounds other values in their place, can miss the bound.
Values sent between devices are 32-bit elements; how exact they have to be, the bound alone decides.
No kernel may reach another device: no remote copies, remote signals or barrier semaphores. Data moves between devices by JAX's collectives and lax.ppermute only.
A program may use at most 128 MiB of HBM per device.

v0:
```python
import jax
import jax.numpy as jnp
from jax import lax
from jax.sharding import PartitionSpec as P

HD = 64
EPSILON = 1e-12


def normalize(hidden):
    center = hidden - jnp.mean(hidden, -1, keepdims=True)
    factor = lax.rsqrt(jnp.mean(center * center, -1, keepdims=True) + EPSILON)
    return (center * factor, factor[:, 0])


def norm_back(upstream, normed, factor, gain):
    scaled = upstream * gain
    inner_mean = jnp.mean(scaled, -1, keepdims=True)
    cross_mean = jnp.mean(scaled * normed, -1, keepdims=True)
    return factor[:, None] * (scaled - inner_mean - normed * cross_mean)


def gelu_exact(inner):
    return jax.nn.gelu(inner, approximate=False)


def masked_scores(queries, key_rows, length):
    scores = jnp.einsum(
        "qhe,khe->hqk", queries, key_rows, preferred_element_type=jnp.float32
    ) * HD ** (-0.5)
    visible = jnp.arange(key_rows.shape[0]) < length
    return jnp.where(visible[None, None, :], scores, -1e30)


def attend(queries, key_rows, value_rows, length):
    scores = masked_scores(queries, key_rows, length)
    largest = jnp.max(scores, -1, keepdims=True)
    weights_exp = jnp.exp(scores - largest)
    total = jnp.sum(weights_exp, -1, keepdims=True)
    probs = weights_exp / total
    mixed = jnp.einsum(
        "hqk,khe->qhe", probs.astype(jnp.bfloat16), value_rows, preferred_element_type=jnp.float32
    )
    log_total = largest[..., 0] + jnp.log(total[..., 0])
    return (mixed.astype(jnp.bfloat16), log_total)


def attend_back(queries, key_rows, value_rows, length, log_total, grad_mixed):
    scores = masked_scores(queries, key_rows, length)
    probs = jnp.exp(scores - log_total[..., None])
    grad_values = jnp.einsum(
        "hqk,qhe->khe", probs.astype(jnp.bfloat16), grad_mixed, preferred_element_type=jnp.float32
    )
    grad_probs = jnp.einsum(
        "qhe,khe->hqk", grad_mixed, value_rows, preferred_element_type=jnp.float32
    )
    centered = jnp.sum(probs * grad_probs, -1, keepdims=True)
    grad_scores = (probs * (grad_probs - centered)).astype(jnp.bfloat16)
    grad_queries = jnp.einsum(
        "hqk,khe->qhe", grad_scores, key_rows, preferred_element_type=jnp.float32
    ) * HD ** (-0.5)
    grad_keys = jnp.einsum(
        "hqk,qhe->khe", grad_scores, queries, preferred_element_type=jnp.float32
    ) * HD ** (-0.5)
    return (grad_queries, grad_keys, grad_values)


def forward_pair(item_tuple):
    pair_q, pair_k, pair_v, length = item_tuple
    return attend(pair_q, pair_k, pair_v, length)


def backward_pair(item_tuple):
    pair_q, pair_k, pair_v, length, pair_lse, pair_grad = item_tuple
    return attend_back(pair_q, pair_k, pair_v, length, pair_lse, pair_grad)


def on_device(
    short_tokens,
    short_lengths,
    long_tokens,
    long_lengths,
    w_qkv,
    b_qv,
    w_out,
    res_biases,
    ln_gains,
    ln_shifts,
    w_up,
    b_up,
    w_down,
    short_cotangent,
    long_cotangent,
):
    short_pairs, short_slot, model_width = short_tokens.shape
    long_pairs, long_slot = (long_tokens.shape[0], long_tokens.shape[1])
    short_rows = short_pairs * short_slot
    long_rows = long_pairs * long_slot
    local_width = w_qkv.shape[2]
    heads_here = b_qv.shape[1]
    head_size = b_qv.shape[2]
    flat = jnp.concatenate(
        [
            short_tokens.reshape(short_rows, model_width),
            long_tokens.reshape(long_rows, model_width),
        ],
        0,
    )
    flat_float = flat.astype(jnp.float32)
    gain_rows = ln_gains.astype(jnp.float32)
    shift_rows = ln_shifts.astype(jnp.float32)
    bias_float = res_biases.astype(jnp.float32)
    projected = jnp.einsum("rd,cde->cre", flat, w_qkv, preferred_element_type=jnp.float32)
    bias_rows = jnp.stack(
        [
            b_qv[0].reshape(local_width).astype(jnp.float32),
            jnp.zeros((local_width,), jnp.float32),
            b_qv[1].reshape(local_width).astype(jnp.float32),
        ]
    )
    projected = (projected + bias_rows[:, None, :]).astype(jnp.bfloat16)
    short_proj = projected[:, :short_rows].reshape(
        3, short_pairs, short_slot, heads_here, head_size
    )
    long_proj = projected[:, short_rows:].reshape(3, long_pairs, long_slot, heads_here, head_size)
    short_att, short_lse = lax.map(
        forward_pair, (short_proj[0], short_proj[1], short_proj[2], short_lengths)
    )
    long_att, long_lse = lax.map(
        forward_pair, (long_proj[0], long_proj[1], long_proj[2], long_lengths)
    )
    mixed = jnp.concatenate(
        [short_att.reshape(short_rows, local_width), long_att.reshape(long_rows, local_width)], 0
    )
    attn_part = jnp.dot(mixed, w_out, preferred_element_type=jnp.float32)
    attn_total = lax.psum(attn_part, "tensor")
    normed_one, factor_one = normalize(flat_float + attn_total + bias_float[0])
    first_out = normed_one * gain_rows[0] + shift_rows[0]
    first_low = first_out.astype(jnp.bfloat16)
    inner = jnp.dot(first_low, w_up, preferred_element_type=jnp.float32) + b_up[0].astype(
        jnp.float32
    )
    activated = gelu_exact(inner).astype(jnp.bfloat16)
    ffn_part = jnp.dot(activated, w_down, preferred_element_type=jnp.float32)
    ffn_total = lax.psum(ffn_part, "tensor")
    normed_two, factor_two = normalize(first_out + ffn_total + bias_float[1])
    encoded = (normed_two * gain_rows[1] + shift_rows[1]).astype(jnp.bfloat16)
    upstream = jnp.concatenate(
        [
            short_cotangent.reshape(short_rows, model_width),
            long_cotangent.reshape(long_rows, model_width),
        ],
        0,
    ).astype(jnp.float32)
    grad_second = norm_back(upstream, normed_two, factor_two, gain_rows[1])
    small_second = jnp.stack(
        [jnp.sum(grad_second, 0), jnp.sum(upstream * normed_two, 0), jnp.sum(upstream, 0)]
    )
    grad_branch = grad_second.astype(jnp.bfloat16)
    grad_down = jnp.einsum("rf,rd->fd", activated, grad_branch, preferred_element_type=jnp.float32)
    grad_activated = jnp.einsum(
        "rd,fd->rf", grad_branch, w_down, preferred_element_type=jnp.float32
    )
    ignored_value, gelu_pullback = jax.vjp(gelu_exact, inner)
    grad_inner = gelu_pullback(grad_activated)[0].astype(jnp.bfloat16)
    grad_up = jnp.einsum("rd,rf->df", first_low, grad_inner, preferred_element_type=jnp.float32)
    grad_up_bias = jnp.sum(grad_inner.astype(jnp.float32), 0)[None, :]
    input_part = jnp.einsum("rf,df->rd", grad_inner, w_up, preferred_element_type=jnp.float32)
    up_shard, down_shard, up_bias_shard, small_second_shard = (
        lax.psum_scatter(grad_up, "dp", scatter_dimension=0, tiled=True),
        lax.psum_scatter(grad_down, "dp", scatter_dimension=1, tiled=True),
        lax.psum_scatter(grad_up_bias, "dp", scatter_dimension=1, tiled=True),
        lax.psum_scatter(small_second, "dp", scatter_dimension=1, tiled=True),
    )
    grad_first_out = grad_second + lax.psum(input_part, "tensor")
    grad_first = norm_back(grad_first_out, normed_one, factor_one, gain_rows[0])
    small_first = jnp.stack(
        [
            jnp.sum(grad_first, 0),
            jnp.sum(grad_first_out * normed_one, 0),
            jnp.sum(grad_first_out, 0),
        ]
    )
    grad_attn = grad_first.astype(jnp.bfloat16)
    grad_out = jnp.einsum("rl,rd->ld", mixed, grad_attn, preferred_element_type=jnp.float32)
    grad_mixed = jnp.einsum(
        "rd,ld->rl", grad_attn, w_out, preferred_element_type=jnp.float32
    ).astype(jnp.bfloat16)
    short_grad_mixed = grad_mixed[:short_rows].reshape(
        short_pairs, short_slot, heads_here, head_size
    )
    long_grad_mixed = grad_mixed[short_rows:].reshape(long_pairs, long_slot, heads_here, head_size)
    short_gq, short_gk, short_gv = lax.map(
        backward_pair,
        (short_proj[0], short_proj[1], short_proj[2], short_lengths, short_lse, short_grad_mixed),
    )
    long_gq, long_gk, long_gv = lax.map(
        backward_pair,
        (long_proj[0], long_proj[1], long_proj[2], long_lengths, long_lse, long_grad_mixed),
    )
    short_grads = (
        jnp.stack([short_gq, short_gk, short_gv])
        .astype(jnp.bfloat16)
        .reshape(3, short_rows, local_width)
    )
    long_grads = (
        jnp.stack([long_gq, long_gk, long_gv])
        .astype(jnp.bfloat16)
        .reshape(3, long_rows, local_width)
    )
    grad_projected = jnp.concatenate([short_grads, long_grads], 1)
    grad_qkv = jnp.einsum("rd,cre->cde", flat, grad_projected, preferred_element_type=jnp.float32)
    grad_bias_rows = jnp.sum(grad_projected.astype(jnp.float32), 1)
    grad_qv_bias = jnp.stack([grad_bias_rows[0], grad_bias_rows[2]]).reshape(
        2, heads_here, head_size
    )
    token_part = jnp.einsum(
        "cre,cde->rd", grad_projected, w_qkv, preferred_element_type=jnp.float32
    )
    qkv_shard, qv_bias_shard, out_shard, small_first_shard = (
        lax.psum_scatter(grad_qkv, "dp", scatter_dimension=1, tiled=True),
        lax.psum_scatter(grad_qv_bias, "dp", scatter_dimension=2, tiled=True),
        lax.psum_scatter(grad_out, "dp", scatter_dimension=1, tiled=True),
        lax.psum_scatter(small_first, "dp", scatter_dimension=1, tiled=True),
    )
    grad_tokens = grad_first + lax.psum(token_part, "tensor")
    grad_res_biases = jnp.concatenate([small_first_shard[0:1], small_second_shard[0:1]], 0)
    grad_gains = jnp.concatenate([small_first_shard[1:2], small_second_shard[1:2]], 0)
    grad_shifts = jnp.concatenate([small_first_shard[2:3], small_second_shard[2:3]], 0)
    return (
        encoded[:short_rows].reshape(short_pairs, short_slot, model_width),
        encoded[short_rows:].reshape(long_pairs, long_slot, model_width),
        grad_tokens[:short_rows].reshape(short_pairs, short_slot, model_width),
        grad_tokens[short_rows:].reshape(long_pairs, long_slot, model_width),
        qkv_shard,
        qv_bias_shard,
        out_shard,
        grad_res_biases,
        grad_gains,
        grad_shifts,
        up_shard,
        up_bias_shard,
        down_shard,
    )


def solution(mesh):
    return jax.shard_map(
        on_device,
        mesh=mesh,
        in_specs=(
            P("dp", None, None),
            P("dp"),
            P("dp", None, None),
            P("dp"),
            P(None, None, "tensor"),
            P(None, "tensor", None),
            P("tensor", None),
            P(),
            P(),
            P(),
            P(None, "tensor"),
            P("tensor", None),
            P("tensor", None),
            P("dp", None, None),
            P("dp", None, None),
        ),
        out_specs=(
            P("dp", None, None),
            P("dp", None, None),
            P("dp", None, None),
            P("dp", None, None),
            P(None, "dp", "tensor"),
            P(None, "tensor", "dp"),
            P("tensor", "dp"),
            P(None, "dp"),
            P(None, "dp"),
            P(None, "dp"),
            P("dp", "tensor"),
            P("tensor", "dp"),
            P("tensor", "dp"),
        ),
        check_vma=False,
    )
```

profile of v0, /device:TPU:0, one launch (start us, length us, event | category | flops | bytes accessed | tf_op | source)
XLA Modules:
  0.0 1305.4 jit_solution(6530653363544916583)
XLA Ops:
  21.0 15.0 %while.53 = (s32[]{:T(128)}, bf16[3,512,3,64]{1,3,2,0:T(8,128)(2,1)}, f32[3,3,512]{2,1,0:T(4,128)}, bf16[3,512,3,64]{1,3,2,0:T(8,128)(2,1)S(1)}, s32[3]{0:T(128)...) while((s32[]{:T(128)}, bf16[3,512,3,64]{1,3,2,0:T(8,128)(2,1)}, ...), condition=%wide.region_7.8_spmd, body=%wide.region_4.7_spmd.sunk | while | flops 210861056 | bytes 10283621 | solution.py:129
  43.2 5.3 while.52
  50.9 4.7 fusion.137
  58.1 223.2 %all-reduce.6.cloned.1.call-done = f32[2048,768]{1,0:T(8,128)} async-done(((f32[2048,768]{1,0:T(8,128)}), f32[2048,768]{1,0:T(8,128)}) %all-reduce.6.cloned.1.call-update) | async-done | bytes 6291472 | tf_op jit(solution)/shard_map/psum | solution.py:136
  281.3 4.2 fusion.130
  288.2 18.4 %multiply_convert_fusion.2 = (bf16[2048,768]{1,0:T(8,128)(2,1)S(1)}, f32[2048,768]{1,0:T(8,128)}, f32[2048,768]{1,0:T(8,128)}) fusion(f32[768]{0:T(1024)S(1)} %copy-done.32, bf16[2048,768]{1,0:T(8,128)(2,1)S(1)} %fusion.103, bf16[768,768]{1,0:T(8,128)(2,1)S(1)} %copy-done), kind=kOutput, calls=%fused_computation.132 | convolution fusion | flops 2519728128 | bytes 20057088 | tf_op jit(solution)/shard_map/dot_general | solution.py:140
  308.3 4.6 fusion.138
  313.1 221.7 %all-reduce.8.cloned.1.call-done = f32[2048,768]{1,0:T(8,128)} async-done(((f32[2048,768]{1,0:T(8,128)}), f32[2048,768]{1,0:T(8,128)}) %all-reduce.8.cloned.1.call-update) | async-done | bytes 6291472 | tf_op jit(solution)/shard_map/psum | solution.py:145
  534.8 5.7 fusion.128
  542.4 4.6 fusion.97
  547.0 5.8 fusion.126
  552.9 9.5 convert_reduce_fusion.1
  564.2 4.5 fusion.139
  571.6 219.0 %all-reduce.10.cloned.1.call-done = f32[2048,768]{1,0:T(8,128)} async-done(((f32[2048,768]{1,0:T(8,128)}), f32[2048,768]{1,0:T(8,128)}) %all-reduce.10.cloned.1.call-update) | async-done | bytes 6291472 | tf_op jit(solution)/shard_map/psum | solution.py:175
  790.6 8.1 multiply_reduce_fusion.2
  798.8 4.7 fusion.125
  811.8 25.9 %while.55 = (s32[]{:T(128)}, bf16[3,512,3,64]{1,3,2,0:T(8,128)(2,1)}, bf16[3,512,3,64]{1,3,2,0:T(8,128)(2,1)}, bf16[3,512,3,64]{1,3,2,0:T(8,128)(2,1)}, bf16[3,5...) while((s32[]{:T(128)}, ...), condition=%wide.region_24.25_spmd, body=%wide.region_22.24_spmd.sunk | while | flops 510589952 | bytes 35625200 | solution.py:197
  838.7 5.1 fusion.119
  844.2 9.6 while.54
  866.3 5.1 fusion.116
  871.4 4.3 copy.129
  875.7 4.7 reshape.242
  880.5 6.0 convolution_bitcast_fusion.1
  886.5 7.9 fusion.110
  894.8 7.0 fusion.140
  912.1 13.6 %all-reduce = f32[2,3,64]{2,1,0:T(4,128)S(1)} all-reduce(f32[2,3,64]{2,1,0:T(4,128)S(1)} %reshape.234), channel_id=3, replica_groups=mesh['dp'=8,'tensor'=4] {'dp'}, use_global_device_ids=true, to_apply=%region_28.29.clone | all-reduce | flops 384 | bytes 3072
  929.4 8.8 reduce-scatter.25.cloned.1.call-done
  939.8 42.0 %reduce-scatter.23.cloned.1.call-done = f32[96,576]{1,0:T(8,128)} async-done(((f32[768,576]{1,0:T(8,128)}), f32[96,576]{1,0:T(8,128)}) %reduce-scatter.23.cloned.1.call-update) | async-done | bytes 221200
  983.6 223.4 %all-reduce.12.cloned.1.call-done = f32[2048,768]{1,0:T(8,128)} async-done(((f32[2048,768]{1,0:T(8,128)}), f32[2048,768]{1,0:T(8,128)}) %all-reduce.12.cloned.1.call-update) | async-done | bytes 6291472 | tf_op jit(solution)/shard_map/psum | solution.py:226
  1207.0 5.5 add.175
  1216.2 35.8 %reduce-scatter.21.cloned.1.call-done = f32[768,96]{0,1:T(8,128)} async-done(((f32[768,768]{0,1:T(8,128)}), f32[768,96]{0,1:T(8,128)}) %reduce-scatter.21.cloned.1.call-update) | async-done | bytes 294928 | tf_op jit(solution)/shard_map/reduce_scatter | solution.py:171
  1252.0 46.3 %reduce-scatter.19.cloned.1.call-done = f32[96,768]{1,0:T(8,128)} async-done(((f32[768,768]{1,0:T(8,128)}), f32[96,768]{1,0:T(8,128)}) %reduce-scatter.19.cloned.1.call-update) | async-done | bytes 294928 | tf_op jit(solution)/shard_map/reduce_scatter | solution.py:170
  (326 shorter events, 135.1 us)
Async XLA Ops:
  7.2 281.0 %copy-start = (bf16[768,768]{1,0:T(8,128)(2,1)S(1)}, bf16[768,768]{1,0:T(8,128)(2,1)}, u32[]{:S(2)}) copy-start(bf16[768,768]{1,0:T(8,128)(2,1)} %param.33) | copy-start | bytes 3538948
  7.2 274.1 %all-reduce.6.cloned.1.call-start = ((), (), s32[]{:S(2)}) async-start(), calls=%async_computation.7 | async-start | bytes 12582912 | tf_op jit(solution)/shard_map/psum | solution.py:136
  12.8 8.1 copy-start.40
  21.0 20.5 %copy-start.16 = (bf16[1,512,192]{1,2,0:T(8,128)(2,1)S(1)}, bf16[1,512,192]{1,2,0:T(8,128)(2,1)}, u32[]{:S(2)}) copy-start(bf16[1,512,192]{1,2,0:T(8,128)(2,1)} %get-tuple-element.455) | copy-start | bytes 589828
  21.0 22.1 %copy-start.42 = (s32[2]{0:T(128)S(1)}, s32[2]{0:T(128)}, u32[]{:S(2)}) copy-start(s32[2]{0:T(128)} %param.24) | copy-start | bytes 28
  36.0 7.1 copy-start.6
  48.5 7.1 copy-start.23
  55.6 479.2 %all-reduce.8.cloned.1.call-start = ((), (), s32[]{:S(2)}) async-start(), calls=%async_computation.8 | async-start | bytes 12582912 | tf_op jit(solution)/shard_map/psum | solution.py:145
  288.2 18.5 %copy-start.9 = (bf16[2048,768]{1,0:T(8,128)(2,1)}, bf16[2048,768]{1,0:T(8,128)(2,1)S(1)}, u32[]{:S(2)}) copy-start(bf16[2048,768]{1,0:T(8,128)(2,1)S(1)} %fusion.103) | copy-start | bytes 9437188
  288.2 20.2 %copy-start.38 = (bf16[768,768]{1,0:T(8,128)(2,1)S(1)}, bf16[768,768]{1,0:T(8,128)(2,1)}, u32[]{:S(2)}) copy-start(bf16[768,768]{1,0:T(8,128)(2,1)} %param.35) | copy-start | bytes 3538948
  312.9 477.7 %all-reduce.10.cloned.1.call-start = ((), (), s32[]{:S(2)}) async-start(), calls=%async_computation.9 | async-start | bytes 12582912 | tf_op jit(solution)/shard_map/psum | solution.py:175
  542.4 10.5 slice-start.1
  552.9 9.5 copy-start.4
  568.7 221.9 %copy-start.22 = (f32[768]{0:T(1024)S(1)}, f32[768]{0:T(1024)}, u32[]{:S(2)}) copy-start(f32[768]{0:T(1024)} %get-tuple-element.469) | copy-start | bytes 9220
  568.7 339.6 %reduce-scatter.31.cloned.1.call-start = ((), (), s32[]{:S(2)}) async-start(), calls=%async_computation.17 | async-start | bytes 442368
  570.3 339.4 %reduce-scatter.29.cloned.1.call-start = ((), (), s32[]{:S(2)}) async-start(), calls=%async_computation.16 | async-start | bytes 442368
  571.4 355.0 %reduce-scatter.27.cloned.1.call-start = ((), (), s32[]{:S(2)}) async-start(), calls=%async_computation.15 | async-start | bytes 442368
  798.8 7.4 copy-start.12
  803.5 8.3 copy-start.41
  837.7 6.6 copy-start.11
  837.7 6.6 copy-start.24
  837.7 6.6 copy-start.43
  838.7 99.5 %reduce-scatter.25.cloned.1.call-start = ((), (), s32[]{:S(2)}) async-start(), calls=%async_computation.14 | async-start | bytes 884736
  843.9 137.8 %reduce-scatter.23.cloned.1.call-start = ((), (), s32[]{:S(2)}) async-start(), calls=%async_computation.13 | async-start | bytes 2211840
  853.8 12.5 copy-start.13
  871.4 9.0 copy-start.14
  871.4 9.0 copy-start.15
  880.4 326.6 %all-reduce.12.cloned.1.call-start = ((), (), s32[]{:S(2)}) async-start(), calls=%async_computation.10 | async-start | bytes 12582912 | tf_op jit(solution)/shard_map/psum | solution.py:226
  886.5 365.6 %reduce-scatter.21.cloned.1.call-start = ((), (), s32[]{:S(2)}) async-start(), calls=%async_computation.12 | async-start | bytes 2654208 | tf_op jit(solution)/shard_map/reduce_scatter | solution.py:171
  894.5 7.3 copy-start.44
  894.5 403.9 %reduce-scatter.19.cloned.1.call-start = ((), (), s32[]{:S(2)}) async-start(), calls=%async_computation.11 | async-start | bytes 2654208 | tf_op jit(solution)/shard_map/reduce_scatter | solution.py:170
  1207.0 91.4 %copy-start.1 = (bf16[768,768]{1,0:T(8,128)(2,1)S(1)}, bf16[768,768]{1,0:T(8,128)(2,1)}, u32[]{:S(2)}) copy-start(bf16[768,768]{1,0:T(8,128)(2,1)} %param.33) | copy-start | bytes 3538948
  (37 other events, 80.8 us)
Sparse Core Ops, SparseCore 0:
  55.7 225.5 all-reduce.5
  313.0 221.7 all-reduce.7
  568.9 221.7 all-reduce.9
  793.5 32.7 reduce-scatter.30
  829.3 33.8 reduce-scatter.28
  866.1 33.8 reduce-scatter.26
  903.2 34.9 reduce-scatter.24
  941.6 40.1 reduce-scatter.22
  984.1 222.8 all-reduce.11
  1210.8 41.2 reduce-scatter.20
  1256.0 42.3 reduce-scatter.18
where the time goes:
time: 1310 us
  waiting for transfers between devices  1020 us (78%)
  matrix products  109 us (8%)
  local copies, waits for them, and re-layouts  84.2 us (6%)
  other arithmetic  59.6 us (5%)
  between operations  15.9 us (1%)
  blocking collectives  13.6 us (1%)
    psum x1, waiting for transfers between devices, on_device(): grad_tokens = grad_first + lax.psum(token_part, 'tensor')  223 us
    psum x1, waiting for transfers between devices, on_device(): attn_total = lax.psum(attn_part, 'tensor')  223 us
    psum x1, waiting for transfers between devices, on_device(): ffn_total = lax.psum(ffn_part, 'tensor')  222 us
    psum x1, waiting for transfers between devices, on_device(): grad_first_out = grad_second + lax.psum(input_part, 'tensor')  219 us
    unnamed x16, waiting for transfers between devices  50.9 us
    reduce_scatter x1, waiting for transfers between devices, on_device(): lax.psum_scatter(grad_up, 'dp', scatter_dimension=0, tiled=True)  46.3 us
    reduce_scatter x1, waiting for transfers between devices, on_device(): lax.psum_scatter(grad_down, 'dp', scatter_dimension=1, tiled=True)  35.8 us
    unnamed x111, local copies, waits for them, and re-layouts  27.9 us
  transfers between devices with their start and end apart: 11, of which 8 were waited for; matrix products, arithmetic and copies ran while one was open for 10% of the time, Pallas kernels for 0%

commit v1 on v0

--- a/solution.py
+++ b/solution.py
@@ -1,3 +1,4 @@
+import functools
 import jax
 import jax.numpy as jnp
 from jax import lax
@@ -5,6 +6,28 @@
 
 HD = 64
 EPSILON = 1e-12
+
+
+def _turn_desk(buf, net_axis):
+    amount_of = lax.axis_size(net_axis)
+
+    def list_lanes(x_new, q_next):
+        if q_next >= amount_of:
+            return x_new
+        row_out = list_lanes(
+            x_new
+            + lax.ppermute(
+                x_new, axis_name=net_axis, perm=[(kk, kk ^ q_next) for kk in range(amount_of)]
+            ),
+            2 * q_next,
+        )
+        return row_out
+
+    latest = list_lanes(buf, 1)
+    return latest
+
+
+number_the_cube = functools.partial(_turn_desk, net_axis="tensor")
 
 
 def normalize(hidden):
@@ -133,7 +156,7 @@
         [short_att.reshape(short_rows, local_width), long_att.reshape(long_rows, local_width)], 0
     )
     attn_part = jnp.dot(mixed, w_out, preferred_element_type=jnp.float32)
-    attn_total = lax.psum(attn_part, "tensor")
+    attn_total = number_the_cube(attn_part)
     normed_one, factor_one = normalize(flat_float + attn_total + bias_float[0])
     first_out = normed_one * gain_rows[0] + shift_rows[0]
     first_low = first_out.astype(jnp.bfloat16)

time: 1310 us -> 1500 us (1.15)
  waiting for transfers between devices: 1020 us -> 1210 us
    ppermute x0 -> x2, waiting for transfers between devices: none -> 405 us  [list_lanes(): lax.ppermute(x_new, axis_name=net_axis, perm=[(kk, kk ^ q_next) for kk in...]
    psum x1 -> x0, waiting for transfers between devices: 223 us -> none  [on_device(): attn_total = lax.psum(attn_part, 'tensor')]
    unnamed x16 -> x15, waiting for transfers between devices: 50.9 us -> 52.4 us
  transfers between devices with their start and end apart: 11 -> 12, of which waited for: 8 -> 9; matrix products, arithmetic and copies ran while one was open for 10% -> 9% of each run, Pallas kernels for 0% -> 0%
where the time goes in v1:
time: 1500 us; the launch traced here: 1490 us
  waiting for transfers between devices  1210 us (81%)
  matrix products  106 us (7%)
  local copies, waits for them, and re-layouts  80.3 us (5%)
  other arithmetic  59.3 us (4%)
  between operations  16.2 us (1%)
    ppermute x2, waiting for transfers between devices, list_lanes(): lax.ppermute(x_new, axis_name=net_axis, perm=[(kk, kk ^ q_next) for kk in...  405 us
    psum x1, waiting for transfers between devices, on_device(): ffn_total = lax.psum(ffn_part, 'tensor')  224 us
    psum x1, waiting for transfers between devices, on_device(): grad_tokens = grad_first + lax.psum(token_part, 'tensor')  223 us
    psum x1, waiting for transfers between devices, on_device(): grad_first_out = grad_second + lax.psum(input_part, 'tensor')  220 us
    unnamed x15, waiting for transfers between devices  52.4 us
    reduce_scatter x1, waiting for transfers between devices, on_device(): lax.psum_scatter(grad_up, 'dp', scatter_dimension=0, tiled=True)  46.2 us
    reduce_scatter x1, waiting for transfers between devices, on_device(): lax.psum_scatter(grad_down, 'dp', scatter_dimension=1, tiled=True)  36 us
  transfers between devices with their start and end apart: 12, of which 9 were waited for; matrix products, arithmetic and copies ran while one was open for 9% of the time, Pallas kernels for 0%

profile of v1, /device:TPU:0, one launch (start us, length us, event | category | flops | bytes accessed | tf_op | source)
XLA Modules:
  0.0 1489.8 jit_solution(8350951096529718978)
XLA Ops:
  8.3 4.1 fusion.122
  21.1 15.0 %while.53 = (s32[]{:T(128)}, bf16[3,512,3,64]{1,3,2,0:T(8,128)(2,1)}, f32[3,3,512]{2,1,0:T(4,128)}, bf16[3,512,3,64]{1,3,2,0:T(8,128)(2,1)S(1)}, s32[3]{0:T(128)...) while((s32[]{:T(128)}, bf16[3,512,3,64]{1,3,2,0:T(8,128)(2,1)}, ...), condition=%wide.region_7.8_spmd, body=%wide.region_4.7_spmd.sunk | while | flops 210861056 | bytes 10283621 | solution.py:152
  42.3 5.3 while.52
  55.4 135.6 %collective-permute-done = f32[2048,768]{1,0:T(8,128)} collective-permute-done((f32[2048,768]{1,0:T(8,128)S(1)}, f32[2048,768]{1,0:T(8,128)}, u32[]{:S(2)}, u32[]{:S(2)}) %collective-permute-start) | collective-permute-done | bytes 6291488 | tf_op jit(solution)/shard_map/ppermute | solution.py:19
  191.0 4.1 add.158
  198.0 269.5 %collective-permute-done.1 = f32[2048,768]{1,0:T(8,128)S(1)} collective-permute-done((f32[2048,768]{1,0:T(8,128)S(1)}, f32[2048,768]{1,0:T(8,128)S(1)}, u32[]{:S(2)}, u32[]{:S(2)}) %collective-permute-start.1) | collective-permute-done | bytes 6291488 | tf_op jit(solution)/shard_map/ppermute | solution.py:19
  471.6 18.4 %multiply_convert_fusion.2 = (bf16[2048,768]{1,0:T(8,128)(2,1)S(1)}, f32[2048,768]{1,0:T(8,128)}, f32[2048,768]{1,0:T(8,128)}) fusion(f32[768]{0:T(1024)S(1)} %convert_reduce_fusion.3, bf16[2048,768]{1,0:T(8,128)(2,1)S(1)} %fusion.103, bf16[768,768]{1,0:T(8,128)(2,1)S(1)} %copy-done), kind=kOutput, calls=%fused_computation.132 | convolution fusion | flops 2519728128 | bytes 20057088 | tf_op jit(solution)/shard_map/dot_general | solution.py:163
  491.7 4.7 fusion.138
  496.5 224.0 %all-reduce.5.cloned.1.call-done = f32[2048,768]{1,0:T(8,128)} async-done(((f32[2048,768]{1,0:T(8,128)}), f32[2048,768]{1,0:T(8,128)}) %all-reduce.5.cloned.1.call-update) | async-done | bytes 6291472 | tf_op jit(solution)/shard_map/psum | solution.py:168
  720.5 5.7 fusion.128
  732.1 5.3 fusion.126
  737.4 9.0 convert_reduce_fusion.1
  748.1 4.5 fusion.139
  754.9 219.7 %all-reduce.7.cloned.1.call-done = f32[2048,768]{1,0:T(8,128)} async-done(((f32[2048,768]{1,0:T(8,128)}), f32[2048,768]{1,0:T(8,128)}) %all-reduce.7.cloned.1.call-update) | async-done | bytes 6291472 | tf_op jit(solution)/shard_map/psum | solution.py:198
  974.6 8.3 multiply_reduce_fusion.2
  983.0 4.7 fusion.125
  996.0 25.9 %while.55 = (s32[]{:T(128)}, bf16[3,512,3,64]{1,3,2,0:T(8,128)(2,1)}, bf16[3,512,3,64]{1,3,2,0:T(8,128)(2,1)}, bf16[3,512,3,64]{1,3,2,0:T(8,128)(2,1)}, bf16[3,5...) while((s32[]{:T(128)}, ...), condition=%wide.region_23.24_spmd, body=%wide.region_21.23_spmd.sunk | while | flops 510589952 | bytes 35625200 | solution.py:220
  1022.9 5.1 fusion.119
  1028.2 9.9 while.54
  1049.1 5.0 fusion.116
  1054.2 4.2 copy.129
  1058.4 4.7 reshape.242
  1063.1 6.0 convolution_bitcast_fusion.1
  1069.2 8.0 fusion.110
  1077.6 7.0 fusion.140
  1094.9 13.4 all-reduce
  1111.9 10.3 reduce-scatter.25.cloned.1.call-done
  1123.8 42.0 %reduce-scatter.23.cloned.1.call-done = f32[96,576]{1,0:T(8,128)} async-done(((f32[768,576]{1,0:T(8,128)}), f32[96,576]{1,0:T(8,128)}) %reduce-scatter.23.cloned.1.call-update) | async-done | bytes 221200
  1167.7 223.4 %all-reduce.9.cloned.1.call-done = f32[2048,768]{1,0:T(8,128)} async-done(((f32[2048,768]{1,0:T(8,128)}), f32[2048,768]{1,0:T(8,128)}) %all-reduce.9.cloned.1.call-update) | async-done | bytes 6291472 | tf_op jit(solution)/shard_map/psum | solution.py:249
  1391.0 5.5 add.181
  1400.3 36.0 %reduce-scatter.21.cloned.1.call-done = f32[768,96]{0,1:T(8,128)} async-done(((f32[768,768]{0,1:T(8,128)}), f32[768,96]{0,1:T(8,128)}) %reduce-scatter.21.cloned.1.call-update) | async-done | bytes 294928 | tf_op jit(solution)/shard_map/reduce_scatter | solution.py:194
  1436.3 46.2 %reduce-scatter.19.cloned.1.call-done = f32[96,768]{1,0:T(8,128)} async-done(((f32[768,768]{1,0:T(8,128)}), f32[96,768]{1,0:T(8,128)}) %reduce-scatter.19.cloned.1.call-update) | async-done | bytes 294928 | tf_op jit(solution)/shard_map/reduce_scatter | solution.py:193
  (314 shorter events, 138.5 us)
Async XLA Ops:
  7.2 464.4 %copy-start = (bf16[768,768]{1,0:T(8,128)(2,1)S(1)}, bf16[768,768]{1,0:T(8,128)(2,1)}, u32[]{:S(2)}) copy-start(bf16[768,768]{1,0:T(8,128)(2,1)} %param.33) | copy-start | bytes 3538948
  7.2 713.3 %all-reduce.5.cloned.1.call-start = ((), (), s32[]{:S(2)}) async-start(), calls=%async_computation.7 | async-start | bytes 12582912 | tf_op jit(solution)/shard_map/psum | solution.py:168
  12.8 8.2 copy-start.34
  21.0 17.8 %copy-start.21 = (bf16[1,512,192]{1,2,0:T(8,128)(2,1)S(1)}, bf16[1,512,192]{1,2,0:T(8,128)(2,1)}, u32[]{:S(2)}) copy-start(bf16[1,512,192]{1,2,0:T(8,128)(2,1)} %get-tuple-element.457) | copy-start | bytes 589828
  21.0 19.5 %copy-start.20 = (bf16[1,512,192]{1,2,0:T(8,128)(2,1)S(1)}, bf16[1,512,192]{1,2,0:T(8,128)(2,1)}, u32[]{:S(2)}) copy-start(bf16[1,512,192]{1,2,0:T(8,128)(2,1)} %get-tuple-element.456) | copy-start | bytes 589828
  21.0 21.1 %copy-start.19 = (bf16[1,512,192]{1,2,0:T(8,128)(2,1)S(1)}, bf16[1,512,192]{1,2,0:T(8,128)(2,1)}, u32[]{:S(2)}) copy-start(bf16[1,512,192]{1,2,0:T(8,128)(2,1)} %get-tuple-element.455) | copy-start | bytes 589828
  21.1 21.2 %copy-start.35 = (s32[2]{0:T(128)S(1)}, s32[2]{0:T(128)}, u32[]{:S(2)}) copy-start(s32[2]{0:T(128)} %param.24) | copy-start | bytes 28
  52.2 145.7 %copy-start.29 = (bf16[2,768]{1,0:T(2,128)(2,1)S(1)}, bf16[2,768]{1,0:T(2,128)(2,1)}, u32[]{:S(2)}) copy-start(bf16[2,768]{1,0:T(2,128)(2,1)} %param.30) | copy-start | bytes 9220
  52.2 145.7 %copy-start.30 = (bf16[2,768]{1,0:T(2,128)(2,1)S(1)}, bf16[2,768]{1,0:T(2,128)(2,1)}, u32[]{:S(2)}) copy-start(bf16[2,768]{1,0:T(2,128)(2,1)} %param.31) | copy-start | bytes 9220
  52.2 145.7 %copy-start.31 = (bf16[2,768]{1,0:T(2,128)(2,1)S(1)}, bf16[2,768]{1,0:T(2,128)(2,1)}, u32[]{:S(2)}) copy-start(bf16[2,768]{1,0:T(2,128)(2,1)} %param.32) | copy-start | bytes 9220
  52.2 145.7 %copy-start.28 = (bf16[1,768]{1,0:T(2,128)(2,1)S(1)}, bf16[1,768]{1,0:T(2,128)(2,1)}, u32[]{:S(2)}) copy-start(bf16[1,768]{1,0:T(2,128)(2,1)} %param.34) | copy-start | bytes 4612
  52.2 415.3 %copy-start.16 = (bf16[3,512,768]{2,1,0:T(8,128)(2,1)S(1)}, bf16[3,512,768]{2,1,0:T(8,128)(2,1)}, u32[]{:S(2)}) copy-start(bf16[3,512,768]{2,1,0:T(8,128)(2,1)} %param.25) | copy-start | bytes 7077892
  52.2 415.3 %copy-start.18 = (bf16[2,256,768]{2,1,0:T(8,128)(2,1)S(1)}, bf16[2,256,768]{2,1,0:T(8,128)(2,1)}, u32[]{:S(2)}) copy-start(bf16[2,256,768]{2,1,0:T(8,128)(2,1)} %param.23) | copy-start | bytes 2359300
  52.2 138.7 %collective-permute-start = (f32[2048,768]{1,0:T(8,128)S(1)}, f32[2048,768]{1,0:T(8,128)}, u32[]{:S(2)}, u32[]{:S(2)}) collective-permute-start(f32[2048,768]{1,0:T(8,128)S(1)} %fusion.137), channel_id=1, source_target_pairs={{0,1},{1,0},{2,3},{3,2},{4,5},{5,4},{6,7},{7,6},{8,9},{9,8},{10,11... | collective-permute-start | bytes 18874376 | tf_op jit(solution)/shard_map/ppermute | solution.py:19
  195.1 272.5 %collective-permute-start.1 = (f32[2048,768]{1,0:T(8,128)S(1)}, f32[2048,768]{1,0:T(8,128)S(1)}, u32[]{:S(2)}, u32[]{:S(2)}) collective-permute-start(f32[2048,768]{1,0:T(8,128)S(1)} %add.158), channel_id=1, source_target_pairs={{0,2},{1,3},{2,0},{3,1},{4,6},{5,7},{6,4},{7,5},{8,10},{9,11},{10,... | collective-permute-start | bytes 18874376 | tf_op jit(solution)/shard_map/ppermute | solution.py:19
  471.6 18.4 %copy-start.13 = (bf16[2048,768]{1,0:T(8,128)(2,1)}, bf16[2048,768]{1,0:T(8,128)(2,1)S(1)}, u32[]{:S(2)}) copy-start(bf16[2048,768]{1,0:T(8,128)(2,1)S(1)} %fusion.103) | copy-start | bytes 9437188
  471.6 20.2 %copy-start.32 = (bf16[768,768]{1,0:T(8,128)(2,1)S(1)}, bf16[768,768]{1,0:T(8,128)(2,1)}, u32[]{:S(2)}) copy-start(bf16[768,768]{1,0:T(8,128)(2,1)} %param.35) | copy-start | bytes 3538948
  496.5 478.1 %all-reduce.7.cloned.1.call-start = ((), (), s32[]{:S(2)}) async-start(), calls=%async_computation.8 | async-start | bytes 12582912 | tf_op jit(solution)/shard_map/psum | solution.py:198
  728.1 9.3 slice-start.1
  737.4 9.0 copy-start.4
  752.7 338.4 %reduce-scatter.31.cloned.1.call-start = ((), (), s32[]{:S(2)}) async-start(), calls=%async_computation.16 | async-start | bytes 442368
  753.8 338.7 %reduce-scatter.29.cloned.1.call-start = ((), (), s32[]{:S(2)}) async-start(), calls=%async_computation.15 | async-start | bytes 442368
  754.8 354.1 %reduce-scatter.27.cloned.1.call-start = ((), (), s32[]{:S(2)}) async-start(), calls=%async_computation.14 | async-start | bytes 442368
  982.9 7.4 copy-start.17
  1021.8 6.3 copy-start.27
  1022.8 99.4 %reduce-scatter.25.cloned.1.call-start = ((), (), s32[]{:S(2)}) async-start(), calls=%async_computation.13 | async-start | bytes 884736
  1028.1 137.7 %reduce-scatter.23.cloned.1.call-start = ((), (), s32[]{:S(2)}) async-start(), calls=%async_computation.12 | async-start | bytes 2211840
  1063.1 328.0 %all-reduce.9.cloned.1.call-start = ((), (), s32[]{:S(2)}) async-start(), calls=%async_computation.9 | async-start | bytes 12582912 | tf_op jit(solution)/shard_map/psum | solution.py:249
  1069.1 367.1 %reduce-scatter.21.cloned.1.call-start = ((), (), s32[]{:S(2)}) async-start(), calls=%async_computation.11 | async-start | bytes 2654208 | tf_op jit(solution)/shard_map/reduce_scatter | solution.py:194
  1077.2 7.3 copy-start.37
  1077.2 405.2 %reduce-scatter.19.cloned.1.call-start = ((), (), s32[]{:S(2)}) async-start(), calls=%async_computation.10 | async-start | bytes 2654208 | tf_op jit(solution)/shard_map/reduce_scatter | solution.py:193
  1391.0 91.4 %copy-start.1 = (bf16[768,768]{1,0:T(8,128)(2,1)S(1)}, bf16[768,768]{1,0:T(8,128)(2,1)}, u32[]{:S(2)}) copy-start(bf16[768,768]{1,0:T(8,128)(2,1)} %param.33) | copy-start | bytes 3538948
  (31 other events, 91.6 us)
Sparse Core Ops, SparseCore 0:
  496.6 223.8 all-reduce.4
  752.8 221.7 all-reduce.6
  977.7 32.7 reduce-scatter.30
  1013.4 33.9 reduce-scatter.28
  1050.2 33.8 reduce-scatter.26
  1087.2 34.9 reduce-scatter.24
  1125.6 40.1 reduce-scatter.22
  1168.2 222.8 all-reduce.8
  1395.0 41.2 reduce-scatter.20
  1440.0 42.3 reduce-scatter.18
